TPU v7x, 32 devices: a whole 2x2x4 slice. The times are simulated.
32 devices in a mesh: section: 4 (over z), dom: 4 (over y, x), ens: 2 (over core).
Axes of the slice: x: 2, y: 2, z: 4, core: 2. Of those that a mesh axis runs over, the one named last changes fastest.
Arguments:
- members: bfloat16 [8, 512, 512], P(('section', 'ens'), 'dom'), may hold values from -6 to 6
- layer_mats: bfloat16 [4, 6, 512, 512], P('section'), may hold values from -0.25 to 0.25
- biases: float32 [4, 2, 512], P('section'), may hold values from -3 to 3
- norm_gains: float32 [4, 2, 512], P('section'), may hold values from 0.25 to 1.75
- edge_blocks: int32 [4, 6], P('dom'), may hold values from 0 to 2
- edge_shift: int32 [4, 6], P('dom'), may hold values from 0 to 127
Outputs:
- final_state: bfloat16 [8, 512, 512], P(('section', 'ens'), 'dom')
- ens_mean: float32 [512, 512], P('dom')
Inputs may be any that keep to these rules, and one draw needn't show every extreme that they name: `edge_blocks`: a frame of 1 block of the previous part (wrapping around), the part's own 1 block, then 1 block of the next part.
All inputs are finite; a program needn't handle non-finite values.
Results may differ from a plain program's by a relative error of at most 0.022.
Values may be sent and summed in bfloat16 or wider, within the bound.
No kernel may reach another device: no remote copies, remote signals or barrier semaphores. Data moves between devices by JAX's collectives and lax.ppermute only.
A program may use at most 64 MiB of HBM per device.

v0:
```python
import functools

import jax
import jax.numpy as jnp
from jax import lax
from jax.experimental import pallas as pl
from jax.experimental.pallas import tpu as pltpu
from jax.sharding import PartitionSpec as P

BLK = 128
HB = 1
EPSILON = 1e-05
MATS = 6
F32 = jnp.float32
BF16 = jnp.bfloat16
AXES = ("section", "dom", "ens")


def with_halo(x, sides, width):
    for axis, dim in sides:
        devices, length = (lax.axis_size(axis), x.shape[dim])
        up = [(i, (i + 1) % devices) for i in range(devices)]
        down = [(j, i) for i, j in up]
        last = lax.slice_in_dim(x, length - width, length, axis=dim)
        first = lax.slice_in_dim(x, 0, width, axis=dim)
        before = lax.ppermute(last, axis, up)
        after = lax.ppermute(first, axis, down)
        x = jnp.concatenate([before, x, after], axis=dim)
    return x


def from_behind(x, axis, by):
    devices = lax.axis_size(axis)
    return lax.ppermute(x, axis, [(i, (i + by) % devices) for i in range(devices)])


def layer_norm(values):
    average = jnp.mean(values, axis=-1, keepdims=True)
    centred = values - average
    spread = jnp.mean(centred * centred, axis=-1, keepdims=True)
    return centred * lax.rsqrt(spread + EPSILON)


def project(values, weight):
    return jnp.einsum("mnd,de->mne", values, weight, preferred_element_type=jnp.float32)


def fetch_rim(state, send_weight):
    outgoing = project(state, send_weight).astype(jnp.bfloat16)
    extended = with_halo(outgoing, (("dom", 1),), HB * BLK)
    return extended


def update_nodes(state, sender_terms, sender_rows, matrices, bias_pair, gain_pair):
    batch_size, node_count, width_d = state.shape
    slot_count = sender_rows.shape[1]
    receiver_terms = project(state, matrices[1]) + bias_pair[0]
    picked = jnp.take(sender_terms, sender_rows.reshape(-1), axis=1).reshape(
        batch_size, node_count, slot_count, width_d
    )
    pre_act = picked.astype(jnp.float32) + receiver_terms[:, :, None, :]
    hidden = jax.nn.silu(pre_act).astype(jnp.bfloat16)
    edge_out = jnp.einsum("mnkd,de->mnke", hidden, matrices[2], preferred_element_type=jnp.float32)
    messages = jnp.sum(layer_norm(edge_out) * gain_pair[0], axis=2).astype(jnp.bfloat16)
    node_pre = project(state, matrices[3]) + project(messages, matrices[4]) + bias_pair[1]
    node_hidden = jax.nn.silu(node_pre).astype(jnp.bfloat16)
    node_out = project(node_hidden, matrices[5])
    return (state.astype(jnp.float32) + layer_norm(node_out) * gain_pair[1]).astype(jnp.bfloat16)


def in_rounds(members, layer_mats, biases, norm_gains, edge_blocks, edge_shift):
    blocks = edge_blocks.shape[0]
    block_rows = jnp.repeat(edge_blocks, BLK, axis=0)
    row_offsets = jnp.repeat(edge_shift, BLK, axis=0)
    positions = (jnp.arange(blocks * BLK, dtype=jnp.int32) % BLK)[:, None]
    sender_rows = block_rows * BLK + (positions + row_offsets) % BLK
    sections = lax.axis_size("section")
    section_index = lax.axis_index("section")
    matrices = layer_mats[0]
    bias_pair = biases[0]
    gain_pair = norm_gains[0]

    def advance(moment, state):
        anchor = (section_index - moment) % sections
        entry_tick = (sections - anchor) % sections
        active = jnp.logical_and(moment >= entry_tick, moment - entry_tick < sections)
        sender_terms = fetch_rim(state, matrices[0])
        state = lax.cond(
            active,
            lambda: update_nodes(state, sender_terms, sender_rows, matrices, bias_pair, gain_pair),
            lambda: state,
        )
        return from_behind(state, "section", 1)

    final_state = lax.fori_loop(0, 2 * sections, advance, members)
    member_count = final_state.shape[0] * sections * lax.axis_size("ens")
    member_total = lax.psum(
        jnp.sum(final_state.astype(jnp.float32), axis=0).astype(jnp.bfloat16), ("section", "ens")
    ).astype(jnp.float32)
    return (final_state, member_total / member_count)


def silu(v):
    half = 0.5 * v
    return half + half * jnp.tanh(half)


def norm(v):
    scale = 1.0 / v.shape[-1]
    centred = v - jnp.sum(v, axis=-1, keepdims=True) * scale
    spread = jnp.sum(centred * centred, axis=-1, keepdims=True) * scale
    return centred * lax.rsqrt(spread + EPSILON)


def dot(a, b):
    return jnp.dot(a, b, preferred_element_type=F32)


def shifted_block(senders, block, shift):
    width = senders.shape[2]
    base = pl.multiple_of((shift // 8) * 8, 8)
    rest = shift % 8
    rows = senders[block, pl.ds(base, BLK + 8), :].reshape(BLK // 8 + 1, 8, width)
    turned = pltpu.roll(rows, (8 - rest) % 8, 1)
    place = lax.broadcasted_iota(jnp.int32, (1, 8, width), 1)
    return jnp.where(place < 8 - rest, turned[:-1], turned[1:]).reshape(BLK, width)


RIDERS = 16
SECOND = 2


def call(kernel, out_shape, args, spaces, scratch=(), flops=0, **kwargs):
    specs = [pl.BlockSpec(memory_space=x) for x in spaces]
    args = [pltpu.with_memory_space_constraint(x, at) if at == pltpu.HBM else x for x, at in zip(args, spaces)]
    outs = jax.tree.map(lambda _: pl.BlockSpec(memory_space=pltpu.VMEM), out_shape)
    return pl.pallas_call(
        functools.partial(kernel, **kwargs),
        out_shape=out_shape,
        in_specs=specs,
        out_specs=outs,
        scratch_shapes=list(scratch),
        cost_estimate=pl.CostEstimate(flops=flops, bytes_accessed=1 << 20, transcendentals=0),
        compiler_params=pltpu.CompilerParams(vmem_limit_bytes=32 << 20),
    )(*args)


def parcel_kernel(members, blocks, shifts, parcel, lists, words, sems):
    slots = blocks.shape[1]
    copies = [
        pltpu.make_async_copy(blocks, words.at[pl.ds(0, 1), :], sems.at[0]),
        pltpu.make_async_copy(shifts, words.at[pl.ds(8, 1), :], sems.at[1]),
        pltpu.make_async_copy(members, parcel.at[pl.ds(0, BLK), :], sems.at[2]),
    ]
    for copy in copies:
        copy.start()
    lists[...] = jnp.zeros_like(lists)
    copies[0].wait()
    copies[1].wait()
    lists[0:1, 0:slots] = words[0:1].astype(F32)
    lists[8:9, 0:slots] = words[8:9].astype(F32)
    parcel[BLK:] = lists[...].astype(BF16)
    copies[2].wait()


def addends(values):
    rows, rest = [], values
    for _ in range(3):
        head = rest.astype(BF16).astype(F32)
        rows.append(head)
        rest = rest - head
    rows.append(jnp.zeros_like(rest))
    return jnp.concatenate(rows, axis=0).astype(BF16)


def half_kernel(core, mats, biases, gains, half, terms, sems):
    part = half.shape[0] - RIDERS
    at = pl.multiple_of(core[0] * part, BLK)
    copies = [
        pltpu.make_async_copy(biases, terms.at[pl.ds(0, 2), :], sems.at[0]),
        pltpu.make_async_copy(gains, terms.at[pl.ds(2, 2), :], sems.at[1]),
        pltpu.make_async_copy(mats.at[pl.ds(at, part), :], half.at[pl.ds(0, part), :], sems.at[2]),
    ]
    for copy in copies:
        copy.start()
    copies[0].wait()
    copies[1].wait()
    half[part:] = addends(terms[...])
    copies[2].wait()


def layers_kernel(*refs, slots, fresh, given, split):
    place = refs[0]
    refs = refs[1:]
    count = 4 if fresh else 1
    inputs, refs = refs[:count], refs[count:]
    mats, biases, gains = refs[:3]
    refs = refs[3:]
    if given:
        parts, refs = refs[:2], refs[2:]
    outs, refs = (refs[:4], refs[4:]) if split else (refs[:1], refs[1:])
    loaded, own_terms, riders, senders, hidden, words, table, sems = refs[:8]
    width = senders.shape[2]
    nodes = 4 * BLK
    d, e = place[0], place[1]
    part = MATS * width // 4
    half = 2 * part
    plans = [
        [
            pltpu.make_async_copy(mats.at[pl.ds(i * part, part), :], loaded.at[0, pl.ds(i * part, part), :], sems.at[i])
            for i in range(4)
        ]
        + [
            pltpu.make_async_copy(biases, own_terms.at[pl.ds(0, 2), :], sems.at[4]),
            pltpu.make_async_copy(gains, own_terms.at[pl.ds(2, 2), :], sems.at[5]),
        ]
    ]
    if given:
        plans.append(
            [
                pltpu.make_async_copy(
                    x.at[pl.ds(0, half), :],
                    loaded.at[1, pl.ds(pl.multiple_of(row * half, BLK), half), :],
                    sems.at[6 + i],
                )
                for i, (x, row) in enumerate(zip(parts, (e, 1 - e)))
            ]
            + [pltpu.make_async_copy(parts[0].at[pl.ds(half, RIDERS), :], riders, sems.at[8])]
        )
    for copies in plans:
        for copy in copies:
            copy.start()

    if fresh:
        copies = [pltpu.make_async_copy(x, refs[8].at[r], sems.at[10 + r]) for r, x in enumerate(inputs)]
        for copy in copies:
            copy.start()
        for copy in copies:
            copy.wait()
        inputs = [refs[8].at[r] for r in range(4)]
        state = jnp.concatenate([x[0:BLK] for x in inputs], axis=0)
        rows = []
        for r in range(4):
            lists = inputs[r][BLK : BLK + 16].astype(F32).astype(jnp.int32)[:, 0:128]
            sender = ((d ^ r) + lists[0:1] + (4 - HB)) % 4 ^ d
            rows += [sender, lists[8:9]]
        numbers = jnp.concatenate(rows, axis=0)
    else:
        state = inputs[0][0:nodes]
        numbers = inputs[0][nodes:].astype(F32).astype(jnp.int32)[0:8, 0:128]
    words[...] = numbers
    to_scalars = pltpu.make_async_copy(words, table, sems.at[9])
    to_scalars.start()

    for at, copies in enumerate(plans):
        last_layer = at == len(plans) - 1
        if at == 0:
            for i in (0, 1, 4, 5):
                copies[i].wait()
            terms = own_terms[...]
            later = copies[2:4]
        else:
            for copy in copies:
                copy.wait()
            values = riders[...].astype(F32)
            terms = values[0:4] + values[4:8] + values[8:12]
            later = []

        def mat(i):
            return loaded[at, i * width : (i + 1) * width, :]

        sent = dot(state, mat(0)).astype(BF16).astype(F32)
        for b in range(4):
            block = sent[b * BLK : (b + 1) * BLK]
            senders[b, 0:BLK] = block
            senders[b, BLK : 2 * BLK] = block
        received = dot(state, mat(1)) + terms[0:1]
        if at == 0:
            to_scalars.wait()
        collected = []
        for b in range(4):
            for k in range(slots):
                v = shifted_block(senders, table[2 * b, k], table[2 * b + 1, k]) + received[b * BLK : (b + 1) * BLK]
                hidden[b, k * BLK : (k + 1) * BLK] = silu(v).astype(BF16)
            edge = dot(hidden[b], mat(2))
            total = norm(edge[0:BLK])
            for k in range(1, slots):
                total += norm(edge[k * BLK : (k + 1) * BLK])
            collected.append((total * terms[2:3]).astype(BF16))
        messages = jnp.concatenate(collected, axis=0)
        for copy in later:
            copy.wait()
        pre = dot(state, mat(3)) + dot(messages, mat(4)) + terms[1:2]
        node_out = dot(silu(pre).astype(BF16), mat(5))
        state = (state.astype(F32) + norm(node_out) * terms[3:4]).astype(BF16)
        if last_layer and split:
            for b in range(4):
                outs[b][...] = state[b * BLK : (b + 1) * BLK]
        elif last_layer:
            outs[0][0:nodes] = state
            spare = jnp.zeros((16 - 8, 128), F32)
            outs[0][nodes:, 0:128] = jnp.concatenate([numbers.astype(F32), spare], axis=0).astype(BF16)
            outs[0][nodes:, 128:] = jnp.zeros((16, width - 128), BF16)


def run_layers(place, inputs, slots, own, given=None, split=False):
    width = inputs[0].shape[1]
    smem, vmem, hbm = pltpu.SMEM, pltpu.VMEM, pltpu.HBM
    fresh = len(inputs) == 4
    args, spaces = [place] + inputs + list(own), [smem] + [pl.ANY if fresh else vmem] * len(inputs) + [hbm] * 3
    if given:
        args, spaces = args + list(given), spaces + [pl.ANY] * 2
    layers = 1 if given is None else 2
    block = jax.ShapeDtypeStruct((BLK, width), BF16)
    whole = jax.ShapeDtypeStruct((4 * BLK + 16, width), BF16)
    return call(
        layers_kernel,
        [block] * 4 if split else whole,
        args,
        spaces,
        scratch=[
            pltpu.VMEM((layers, MATS * width, width), BF16),
            pltpu.VMEM((4, width), F32),
            pltpu.VMEM((RIDERS, width), BF16),
            pltpu.VMEM((4, 2 * BLK + 8, width), F32),
            pltpu.VMEM((4, slots * BLK, width), BF16),
            pltpu.VMEM((8, 128), jnp.int32),
            pltpu.SMEM((8, 128), jnp.int32),
            pltpu.SemaphoreType.DMA((14,)),
        ]
        + [pltpu.VMEM((4, BLK + 16, width), BF16)] * fresh,
        flops=layers * 2 * 4 * BLK * (slots + 5) * width * width,
        slots=slots,
        fresh=fresh,
        given=given is not None,
        split=split,
    )


def messages_kernel(place, *refs, targets):
    blocks, refs = refs[:4], refs[4:]
    outs, held = refs[:-1], refs[-1]
    total = jnp.zeros(blocks[0].shape, F32)
    for r, block in enumerate(blocks):
        held[r] = block[...]
        total += block[...].astype(F32)
    for out, section in zip(outs, targets):
        out[0:BLK] = held[place[0] ^ section]
        out[BLK:] = total.astype(BF16)


def in_two_stages(members, layer_mats, biases, norm_gains, edge_blocks, edge_shift):
    doms, cores = lax.axis_size("dom"), lax.axis_size("ens")
    layers = lax.axis_size("section")
    s, d, e = (lax.axis_index(a) for a in AXES)
    slots = edge_blocks.shape[1]
    width = members.shape[2]
    mats = layer_mats[0].reshape(MATS * width, width)
    part = MATS * width // 4
    place = jnp.stack([d, e]).astype(jnp.int32)
    smem, vmem = pltpu.SMEM, pltpu.VMEM
    spots = [(i, j, k) for i in range(layers) for j in range(doms) for k in range(cores)]

    def shape(rows):
        return jax.ShapeDtypeStruct((rows, width), BF16)

    def index(i, j, k):
        return (i * doms + j) * cores + k

    def send(x, pairs):
        return lax.ppermute(x, AXES, [(index(*a), index(*b)) for a, b in pairs])

    def swap(x, by):
        a, b, c = by
        return send(x, [((i, j, k), (i ^ a, j ^ b, k ^ c)) for i, j, k in spots])

    def hop(x, source, target):
        return send(x, [((source, j, k), (target, j, k)) for i, j, k in spots if i == source])

    hbm = pltpu.HBM
    parcel = call(
        parcel_kernel,
        shape(BLK + 16),
        (members[0], edge_blocks, edge_shift),
        [hbm] * 3,
        [pltpu.VMEM((16, width), F32), pltpu.VMEM((16, slots), jnp.int32), pltpu.SemaphoreType.DMA((3,))],
    )
    arrived = [
        send(parcel, [((i, i ^ r, k), (0, i, k)) for i in range(layers) for k in range(cores)])
        for r in range(doms)
    ]

    own = (mats, biases[0], norm_gains[0])
    half = call(
        half_kernel,
        shape(2 * part + RIDERS),
        (place[1:], *own),
        [smem] + [hbm] * 3,
        [pltpu.VMEM((4, width), F32), pltpu.SemaphoreType.DMA((3,))],
    )
    half = hop(half, layers - 1, SECOND)

    state = run_layers(place, arrived, slots, own)
    state = hop(state, 0, 1)
    state = run_layers(place, [state], slots, own)
    half = lax.optimization_barrier((half, state))[0]
    given = (half, swap(half, (0, 0, 1)))
    state = hop(state, 1, SECOND)
    blocks = run_layers(place, [state], slots, own, given, split=True)

    columns = [blocks[0]] + [swap(blocks[r], (0, r, 0)) for r in range(1, doms)]
    targets = [i for i in range(layers) if i != SECOND] + [SECOND]
    packed = call(
        messages_kernel,
        [shape(2 * BLK)] * layers,
        (place, *columns),
        [smem] + [vmem] * doms,
        [pltpu.VMEM((doms, BLK, width), BF16)],
        targets=targets,
    )
    final = packed[-1]
    for i, message in zip(targets[:-1], packed):
        final = jnp.where(s == i, hop(message, SECOND, i), final)
    total = final[BLK:]
    total = total.astype(F32) + swap(total, (0, 0, 1)).astype(F32)
    count = members.shape[0] * layers * cores
    return (final[None, :BLK], total / count)


def solution(mesh):
    shape = dict(mesh.shape)
    placed = (
        P(("section", "ens"), "dom", None),
        P("section", None, None, None),
        P("section", None, None),
        P("section", None, None),
        P("dom", None),
        P("dom", None),
    )

    def on_device(members, layer_mats, biases, norm_gains, edge_blocks, edge_shift):
        small = shape["section"] == 4 and shape["dom"] == 4 and shape["ens"] == 2
        one_each = members.shape[:2] == (1, BLK) and layer_mats.shape[0] == 1
        plan = in_two_stages if small and one_each else in_rounds
        return plan(members, layer_mats, biases, norm_gains, edge_blocks, edge_shift)

    return jax.shard_map(
        on_device,
        mesh=mesh,
        in_specs=placed,
        out_specs=(P(("section", "ens"), "dom", None), P("dom", None)),
        check_vma=False,
    )
```

profile of v0, /device:TPU:0, one launch (start us, length us, event | category | flops | bytes accessed | tf_op | source)
XLA Modules:
  0.0 135.1 jit_solution(14168086024925117280)
XLA Ops:
  0.6 1.5 %shard_map.80 = bf16[1552,512]{1,0:T(8,128)(2,1)S(1)} custom-call(s32[1]{0:T(128)} %bitcast.1.core, bf16[3072,512]{1,0:T(8,128)(2,1)} %bitcast.8, f32[2,512]{1,0:T(2,128)} %bitcast.13, f32[2,512]{1,0:T(2,128)} %bitcast.17), custom_call_target="tpu_custom_call" | custom-call | bytes 1048576 | tf_op jit(solution)/shard_map/pallas_call | solution.py:137
  2.1 0.8 collective-permute-start.6
  2.9 1.0 shard_map.77
  3.9 0.7 collective-permute-start
  4.5 1.3 collective-permute-start.1
  5.8 1.3 collective-permute-start.2
  7.1 1.3 collective-permute-start.3
  8.4 0.1 pad_add_fusion.refs_0_.place
  8.5 0.0 collective-permute-done.refs_1_
  8.5 5.5 %collective-permute-done.1.refs_2_ = bf16[144,512]{1,0:T(8,128)(2,1)} collective-permute-done((bf16[144,512]{1,0:T(8,128)(2,1)S(1)}, bf16[144,512]{1,0:T(8,128)(2,1)}, u32[]{:S(2)}, u32[]{:S(2)}) %collective-permute-start.1) | collective-permute-done | bytes 147488 | tf_op jit(solution)/shard_map/ppermute | solution.py:371
  14.0 1.4 %collective-permute-done.2.refs_3_ = bf16[144,512]{1,0:T(8,128)(2,1)} collective-permute-done((bf16[144,512]{1,0:T(8,128)(2,1)S(1)}, bf16[144,512]{1,0:T(8,128)(2,1)}, u32[]{:S(2)}, u32[]{:S(2)}) %collective-permute-start.2) | collective-permute-done | bytes 147488 | tf_op jit(solution)/shard_map/ppermute | solution.py:371
  15.4 4.7 %collective-permute-done.3.refs_4_ = bf16[144,512]{1,0:T(8,128)(2,1)} collective-permute-done((bf16[144,512]{1,0:T(8,128)(2,1)S(1)}, bf16[144,512]{1,0:T(8,128)(2,1)}, u32[]{:S(2)}, u32[]{:S(2)}) %collective-permute-start.3) | collective-permute-done | bytes 147488 | tf_op jit(solution)/shard_map/ppermute | solution.py:371
  20.1 8.5 %shard_map.78 = bf16[528,512]{1,0:T(8,128)(2,1)S(1)} custom-call(s32[2]{0:T(128)S(1)} %pad_add_fusion.refs_0_.place, bf16[144,512]{1,0:T(8,128)(2,1)S(1)} %collective-permute-done.refs_1_, bf16[144,512]{1,0:T(8,128)(2,1)} %collective-permute-done.1.refs_2_, bf16[144,512]{1,0:T(8,128)(2,1)} %collective-permute-done.2.refs_3_, ...), custom_call_target="tpu_custom_call" | custom-call | flops 2952790016 | bytes 1048576 | tf_op jit(solution)/shard_map/pallas_call | solution.py:137
  28.6 1.3 collective-permute-start.4
  29.9 12.0 %collective-permute-done.4.refs_1_ = bf16[528,512]{1,0:T(8,128)(2,1)S(1)} collective-permute-done((bf16[528,512]{1,0:T(8,128)(2,1)S(1)}, bf16[528,512]{1,0:T(8,128)(2,1)S(1)}, u32[]{:S(2)}, u32[]{:S(2)}) %collective-permute-start.4) | collective-permute-done | bytes 540704 | tf_op jit(solution)/shard_map/ppermute | solution.py:371
  41.9 8.1 %shard_map.79 = bf16[528,512]{1,0:T(8,128)(2,1)S(1)} custom-call(s32[2]{0:T(128)S(1)} %pad_add_fusion.refs_0_.place, bf16[528,512]{1,0:T(8,128)(2,1)S(1)} %collective-permute-done.4.refs_1_, bf16[3072,512]{1,0:T(8,128)(2,1)} %bitcast.10, f32[2,512]{1,0:T(2,128)} %bitcast.15, f32[2,512]{1,0:T(2,128)} %bitcast.19), custom_call_target="tpu_custom_call" | custom-call | flops 2952790016 | bytes 1048576 | tf_op jit(solution)/shard_map/pallas_call | solution.py:137
  50.0 0.0 collective-permute-done.6.refs_5_
  50.0 0.1 collective-permute-start.7
  50.1 0.9 collective-permute-start.5
  50.9 0.0 collective-permute-done.5.refs_1_
  51.0 2.5 %collective-permute-done.7.refs_6_ = bf16[1552,512]{1,0:T(8,128)(2,1)S(1)} collective-permute-done((bf16[1552,512]{1,0:T(8,128)(2,1)S(1)}, bf16[1552,512]{1,0:T(8,128)(2,1)S(1)}, u32[]{:S(2)}, u32[]{:S(2)}) %collective-permute-start.7) | collective-permute-done | bytes 1589280 | tf_op jit(solution)/shard_map/ppermute | solution.py:371
  53.5 13.4 %shard_map.81 = (bf16[128,512]{1,0:T(8,128)(2,1)S(1)}, bf16[128,512]{1,0:T(8,128)(2,1)S(1)}, bf16[128,512]{1,0:T(8,128)(2,1)S(1)}, bf16[128,512]{1,0:T(8,128)(2,1)S(1)}) custom-call(s32[2]{0:T(128)S(1)} %pad_add_fusion.refs_0_.place, bf16[528,512]{1,0:T(8,128)(2,1)S(1)} %collective-permute-done.5.refs_1_, bf16[3072,512]{1,0:T(8,128)(2,1)} %bitcast.11, ...), custom_call_target="tpu_custom_call" | custom-call | flops 5905580032 | bytes 1048576 | tf_op jit(solution)/shard_map/pallas_call | solution.py:137
  66.9 29.1 %collective-permute-start.10 = (bf16[128,512]{1,0:T(8,128)(2,1)S(1)}, bf16[128,512]{1,0:T(8,128)(2,1)S(1)}, u32[]{:S(2)}, u32[]{:S(2)}) collective-permute-start(bf16[128,512]{1,0:T(8,128)(2,1)S(1)} %get-tuple-element.15), channel_id=1, source_target_pairs={{0,6},{1,7},{2,4},{3,5},{4,2},{5,3},{6,0},{7,1},{8,14},{9,15},{10,... | collective-permute-start | bytes 393224 | tf_op jit(solution)/shard_map/ppermute | solution.py:371
  96.1 0.0 collective-permute-start.8
  96.1 0.6 collective-permute-start.9
  96.7 3.7 %collective-permute-done.10.refs_3_ = bf16[128,512]{1,0:T(8,128)(2,1)S(1)} collective-permute-done((bf16[128,512]{1,0:T(8,128)(2,1)S(1)}, bf16[128,512]{1,0:T(8,128)(2,1)S(1)}, u32[]{:S(2)}, u32[]{:S(2)}) %collective-permute-start.10) | collective-permute-done | bytes 131104 | tf_op jit(solution)/shard_map/ppermute | solution.py:371
  100.4 1.5 %collective-permute-done.8.refs_1_ = bf16[128,512]{1,0:T(8,128)(2,1)S(1)} collective-permute-done((bf16[128,512]{1,0:T(8,128)(2,1)S(1)}, bf16[128,512]{1,0:T(8,128)(2,1)S(1)}, u32[]{:S(2)}, u32[]{:S(2)}) %collective-permute-start.8) | collective-permute-done | bytes 131104 | tf_op jit(solution)/shard_map/ppermute | solution.py:371
  102.0 0.7 collective-permute-done.9.refs_2_
  102.7 0.7 shard_map.82
  103.4 0.7 collective-permute-start.11
  104.1 0.7 collective-permute-start.12
  104.8 1.3 collective-permute-start.13
  106.1 0.0 collective-permute-done.11
  106.1 0.0 collective-permute-done.12
  106.1 26.2 %collective-permute-done.13 = bf16[256,512]{1,0:T(8,128)(2,1)S(1)} collective-permute-done((bf16[256,512]{1,0:T(8,128)(2,1)S(1)}, bf16[256,512]{1,0:T(8,128)(2,1)S(1)}, u32[]{:S(2)}, u32[]{:S(2)}) %collective-permute-start.13) | collective-permute-done | bytes 262176 | tf_op jit(solution)/shard_map/ppermute | solution.py:371
  132.3 0.7 fusion
  133.0 0.0 collective-permute-start.14
  133.0 1.3 collective-permute-done.14
  134.4 0.7 add_multiply_fusion
  (1 shorter events, 0.0 us)
Async XLA Ops:
  2.1 47.9 %collective-permute-start.6 = (bf16[1552,512]{1,0:T(8,128)(2,1)S(1)}, bf16[1552,512]{1,0:T(8,128)(2,1)S(1)}, u32[]{:S(2)}, u32[]{:S(2)}) collective-permute-start(bf16[1552,512]{1,0:T(8,128)(2,1)S(1)} %shard_map.80), channel_id=1, source_target_pairs={{24,16},{25,17},{26,18},{27,19},{28,20},{29,21},{30,22},{31,23}} | collective-permute-start | bytes 4767752 | tf_op jit(solution)/shard_map/ppermute | solution.py:371
  3.9 4.7 %collective-permute-start = (bf16[144,512]{1,0:T(8,128)(2,1)S(1)}, bf16[144,512]{1,0:T(8,128)(2,1)S(1)}, u32[]{:S(2)}, u32[]{:S(2)}) collective-permute-start(bf16[144,512]{1,0:T(8,128)(2,1)S(1)} %shard_map.77), channel_id=1, source_target_pairs={{0,0},{1,1},{10,2},{11,3},{20,4},{21,5},{30,6},{31,7}} | collective-permute-start | bytes 442376 | tf_op jit(solution)/shard_map/ppermute | solution.py:371
  4.5 9.4 %collective-permute-start.1 = (bf16[144,512]{1,0:T(8,128)(2,1)S(1)}, bf16[144,512]{1,0:T(8,128)(2,1)}, u32[]{:S(2)}, u32[]{:S(2)}) collective-permute-start(bf16[144,512]{1,0:T(8,128)(2,1)S(1)} %shard_map.77), channel_id=1, source_target_pairs={{2,0},{3,1},{8,2},{9,3},{22,4},{23,5},{28,6},{29,7}} | collective-permute-start | bytes 442376 | tf_op jit(solution)/shard_map/ppermute | solution.py:371
  5.8 9.6 %collective-permute-start.2 = (bf16[144,512]{1,0:T(8,128)(2,1)S(1)}, bf16[144,512]{1,0:T(8,128)(2,1)}, u32[]{:S(2)}, u32[]{:S(2)}) collective-permute-start(bf16[144,512]{1,0:T(8,128)(2,1)S(1)} %shard_map.77), channel_id=1, source_target_pairs={{4,0},{5,1},{14,2},{15,3},{16,4},{17,5},{26,6},{27,7}} | collective-permute-start | bytes 442376 | tf_op jit(solution)/shard_map/ppermute | solution.py:371
  7.1 13.0 %collective-permute-start.3 = (bf16[144,512]{1,0:T(8,128)(2,1)S(1)}, bf16[144,512]{1,0:T(8,128)(2,1)}, u32[]{:S(2)}, u32[]{:S(2)}) collective-permute-start(bf16[144,512]{1,0:T(8,128)(2,1)S(1)} %shard_map.77), channel_id=1, source_target_pairs={{6,0},{7,1},{12,2},{13,3},{18,4},{19,5},{24,6},{25,7}} | collective-permute-start | bytes 442376 | tf_op jit(solution)/shard_map/ppermute | solution.py:371
  28.6 13.3 %collective-permute-start.4 = (bf16[528,512]{1,0:T(8,128)(2,1)S(1)}, bf16[528,512]{1,0:T(8,128)(2,1)S(1)}, u32[]{:S(2)}, u32[]{:S(2)}) collective-permute-start(bf16[528,512]{1,0:T(8,128)(2,1)S(1)} %shard_map.78), channel_id=1, source_target_pairs={{0,8},{1,9},{2,10},{3,11},{4,12},{5,13},{6,14},{7,15}} | collective-permute-start | bytes 1622024 | tf_op jit(solution)/shard_map/ppermute | solution.py:371
  50.0 3.5 %collective-permute-start.7 = (bf16[1552,512]{1,0:T(8,128)(2,1)S(1)}, bf16[1552,512]{1,0:T(8,128)(2,1)S(1)}, u32[]{:S(2)}, u32[]{:S(2)}) collective-permute-start(bf16[1552,512]{1,0:T(8,128)(2,1)S(1)} %collective-permute-done.6.refs_5_), channel_id=1, source_target_pairs={{0,1},{1,0},{2,3},{3,2},{4,5},{5,4},{6,7},{7,6},{8,9},{9,8},{10,11... | collective-permute-start | bytes 4767752 | tf_op jit(solution)/shard_map/ppermute | solution.py:371
  50.1 0.9 collective-permute-start.5
  66.9 33.5 %collective-permute-start.10 = (bf16[128,512]{1,0:T(8,128)(2,1)S(1)}, bf16[128,512]{1,0:T(8,128)(2,1)S(1)}, u32[]{:S(2)}, u32[]{:S(2)}) collective-permute-start(bf16[128,512]{1,0:T(8,128)(2,1)S(1)} %get-tuple-element.15), channel_id=1, source_target_pairs={{0,6},{1,7},{2,4},{3,5},{4,2},{5,3},{6,0},{7,1},{8,14},{9,15},{10,... | collective-permute-start | bytes 393224 | tf_op jit(solution)/shard_map/ppermute | solution.py:371
  96.1 5.9 %collective-permute-start.8 = (bf16[128,512]{1,0:T(8,128)(2,1)S(1)}, bf16[128,512]{1,0:T(8,128)(2,1)S(1)}, u32[]{:S(2)}, u32[]{:S(2)}) collective-permute-start(bf16[128,512]{1,0:T(8,128)(2,1)S(1)} %get-tuple-element.13), channel_id=1, source_target_pairs={{0,2},{1,3},{2,0},{3,1},{4,6},{5,7},{6,4},{7,5},{8,10},{9,11},{10,... | collective-permute-start | bytes 393224 | tf_op jit(solution)/shard_map/ppermute | solution.py:371
  96.1 6.6 %collective-permute-start.9 = (bf16[128,512]{1,0:T(8,128)(2,1)S(1)}, bf16[128,512]{1,0:T(8,128)(2,1)S(1)}, u32[]{:S(2)}, u32[]{:S(2)}) collective-permute-start(bf16[128,512]{1,0:T(8,128)(2,1)S(1)} %get-tuple-element.14), channel_id=1, source_target_pairs={{0,4},{1,5},{2,6},{3,7},{4,0},{5,1},{6,2},{7,3},{8,12},{9,13},{10,... | collective-permute-start | bytes 393224 | tf_op jit(solution)/shard_map/ppermute | solution.py:371
  103.4 2.7 %collective-permute-start.11 = (bf16[256,512]{1,0:T(8,128)(2,1)S(1)}, bf16[256,512]{1,0:T(8,128)(2,1)S(1)}, u32[]{:S(2)}, u32[]{:S(2)}) collective-permute-start(bf16[256,512]{1,0:T(8,128)(2,1)S(1)} %get-tuple-element.16), channel_id=1, source_target_pairs={{16,24},{17,25},{18,26},{19,27},{20,28},{21,29},{22,30},{23,31}} | collective-permute-start | bytes 786440 | tf_op jit(solution)/shard_map/ppermute | solution.py:371
  104.1 2.0 %collective-permute-start.12 = (bf16[256,512]{1,0:T(8,128)(2,1)S(1)}, bf16[256,512]{1,0:T(8,128)(2,1)S(1)}, u32[]{:S(2)}, u32[]{:S(2)}) collective-permute-start(bf16[256,512]{1,0:T(8,128)(2,1)S(1)} %get-tuple-element.17), channel_id=1, source_target_pairs={{16,8},{17,9},{18,10},{19,11},{20,12},{21,13},{22,14},{23,15}} | collective-permute-start | bytes 786440 | tf_op jit(solution)/shard_map/ppermute | solution.py:371
  104.8 27.5 %collective-permute-start.13 = (bf16[256,512]{1,0:T(8,128)(2,1)S(1)}, bf16[256,512]{1,0:T(8,128)(2,1)S(1)}, u32[]{:S(2)}, u32[]{:S(2)}) collective-permute-start(bf16[256,512]{1,0:T(8,128)(2,1)S(1)} %get-tuple-element.18), channel_id=1, source_target_pairs={{16,0},{17,1},{18,2},{19,3},{20,4},{21,5},{22,6},{23,7}} | collective-permute-start | bytes 786440 | tf_op jit(solution)/shard_map/ppermute | solution.py:371
  133.0 1.3 collective-permute-start.14
where the time goes:
time: 135 us
  waiting for transfers between devices  59.6 us (44%)
  starting transfers between devices  40 us (30%)
  Pallas kernels  33.1 us (25%)
    ppermute x15, waiting for transfers between devices, send(): return lax.ppermute(x, AXES, [(index(*a), index(*b)) for a, b in pairs])  59.6 us
    ppermute x15, starting transfers between devices, send(): return lax.ppermute(x, AXES, [(index(*a), index(*b)) for a, b in pairs])  40 us
    pallas_call x6, Pallas kernels, call(): pl.pallas_call(functools.partial(kernel, **kwargs), out_shape=out_shape,...  33.1 us
  transfers between devices with their start and end apart: 15, of which 10 were waited for; matrix products, arithmetic and copies ran while one was open for 0% of the time, Pallas kernels for 13%

commit v1 on v0

--- a/solution.py
+++ b/solution.py
@@ -101,7 +101,7 @@
 
 
 def silu(v):
-    half = 0.5 * v
+    half = jnp.asarray(0.5, v.dtype) * v
     return half + half * jnp.tanh(half)
 
 
@@ -189,7 +189,11 @@
     copies[2].wait()
 
 
-def layers_kernel(*refs, slots, fresh, given, split):
+def layers_kernel(*refs, where, **kwargs):
+    pl.when(refs[0][2] == where)(lambda: whole_member(*refs, **kwargs))
+
+
+def whole_member(*refs, slots, fresh, given, split):
     place = refs[0]
     refs = refs[1:]
     count = 4 if fresh else 1
@@ -207,12 +211,12 @@
     half = 2 * part
     plans = [
         [
-            pltpu.make_async_copy(mats.at[pl.ds(i * part, part), :], loaded.at[0, pl.ds(i * part, part), :], sems.at[i])
-            for i in range(4)
+            pltpu.make_async_copy(biases, own_terms.at[pl.ds(0, 2), :], sems.at[14]),
+            pltpu.make_async_copy(gains, own_terms.at[pl.ds(2, 2), :], sems.at[15]),
         ]
         + [
-            pltpu.make_async_copy(biases, own_terms.at[pl.ds(0, 2), :], sems.at[4]),
-            pltpu.make_async_copy(gains, own_terms.at[pl.ds(2, 2), :], sems.at[5]),
+            pltpu.make_async_copy(mats.at[pl.ds(i * width, width), :], loaded.at[0, pl.ds(i * width, width), :], sems.at[i])
+            for i in range(MATS)
         ]
     ]
     if given:
@@ -255,18 +259,21 @@
     for at, copies in enumerate(plans):
         last_layer = at == len(plans) - 1
         if at == 0:
-            for i in (0, 1, 4, 5):
-                copies[i].wait()
+            copies[0].wait()
+            copies[1].wait()
             terms = own_terms[...]
-            later = copies[2:4]
+            matrix_copies = copies[2:]
         else:
             for copy in copies:
                 copy.wait()
             values = riders[...].astype(F32)
             terms = values[0:4] + values[4:8] + values[8:12]
-            later = []
+            matrix_copies = None
 
         def mat(i):
+            if matrix_copies and matrix_copies[i] is not None:
+                matrix_copies[i].wait()
+                matrix_copies[i] = None
             return loaded[at, i * width : (i + 1) * width, :]
 
         sent = dot(state, mat(0)).astype(BF16).astype(F32)
@@ -274,22 +281,20 @@
             block = sent[b * BLK : (b + 1) * BLK]
             senders[b, 0:BLK] = block
             senders[b, BLK : 2 * BLK] = block
-        received = dot(state, mat(1)) + terms[0:1]
+        received = (dot(state, mat(1)) + terms[0:1]).astype(BF16)
         if at == 0:
             to_scalars.wait()
         collected = []
         for b in range(4):
             for k in range(slots):
-                v = shifted_block(senders, table[2 * b, k], table[2 * b + 1, k]) + received[b * BLK : (b + 1) * BLK]
-                hidden[b, k * BLK : (k + 1) * BLK] = silu(v).astype(BF16)
+                v = shifted_block(senders, table[2 * b, k], table[2 * b + 1, k]).astype(BF16)
+                hidden[b, k * BLK : (k + 1) * BLK] = silu(v + received[b * BLK : (b + 1) * BLK])
             edge = dot(hidden[b], mat(2))
             total = norm(edge[0:BLK])
             for k in range(1, slots):
                 total += norm(edge[k * BLK : (k + 1) * BLK])
             collected.append((total * terms[2:3]).astype(BF16))
         messages = jnp.concatenate(collected, axis=0)
-        for copy in later:
-            copy.wait()
         pre = dot(state, mat(3)) + dot(messages, mat(4)) + terms[1:2]
         node_out = dot(silu(pre).astype(BF16), mat(5))
         state = (state.astype(F32) + norm(node_out) * terms[3:4]).astype(BF16)
@@ -303,7 +308,7 @@
             outs[0][nodes:, 128:] = jnp.zeros((16, width - 128), BF16)
 
 
-def run_layers(place, inputs, slots, own, given=None, split=False):
+def run_layers(place, where, inputs, slots, own, given=None, split=False):
     width = inputs[0].shape[1]
     smem, vmem, hbm = pltpu.SMEM, pltpu.VMEM, pltpu.HBM
     fresh = len(inputs) == 4
@@ -326,10 +331,11 @@
             pltpu.VMEM((4, slots * BLK, width), BF16),
             pltpu.VMEM((8, 128), jnp.int32),
             pltpu.SMEM((8, 128), jnp.int32),
-            pltpu.SemaphoreType.DMA((14,)),
+            pltpu.SemaphoreType.DMA((16,)),
         ]
         + [pltpu.VMEM((4, BLK + 16, width), BF16)] * fresh,
         flops=layers * 2 * 4 * BLK * (slots + 5) * width * width,
+        where=where,
         slots=slots,
         fresh=fresh,
         given=given is not None,
@@ -357,7 +363,7 @@
     width = members.shape[2]
     mats = layer_mats[0].reshape(MATS * width, width)
     part = MATS * width // 4
-    place = jnp.stack([d, e]).astype(jnp.int32)
+    place = jnp.stack([d, e, s]).astype(jnp.int32)
     smem, vmem = pltpu.SMEM, pltpu.VMEM
     spots = [(i, j, k) for i in range(layers) for j in range(doms) for k in range(cores)]
 
@@ -394,19 +400,19 @@
     half = call(
         half_kernel,
         shape(2 * part + RIDERS),
-        (place[1:], *own),
+        (place[1:2], *own),
         [smem] + [hbm] * 3,
         [pltpu.VMEM((4, width), F32), pltpu.SemaphoreType.DMA((3,))],
     )
     half = hop(half, layers - 1, SECOND)
 
-    state = run_layers(place, arrived, slots, own)
+    state = run_layers(place, 0, arrived, slots, own)
     state = hop(state, 0, 1)
-    state = run_layers(place, [state], slots, own)
+    state = run_layers(place, 1, [state], slots, own)
     half = lax.optimization_barrier((half, state))[0]
     given = (half, swap(half, (0, 0, 1)))
     state = hop(state, 1, SECOND)
-    blocks = run_layers(place, [state], slots, own, given, split=True)
+    blocks = run_layers(place, SECOND, [state], slots, own, given, split=True)
 
     columns = [blocks[0]] + [swap(blocks[r], (0, r, 0)) for r in range(1, doms)]
     targets = [i for i in range(layers) if i != SECOND] + [SECOND]

time: 135 us -> 134 us (level)
  Pallas kernels: 33.1 us -> 13.3 us
  waiting for transfers between devices: 59.6 us -> 78.3 us
    pallas_call x6, Pallas kernels: 33.1 us -> 13.3 us  [call(): pl.pallas_call(functools.partial(kernel, **kwargs), out_shape=out_shape,...]
    ppermute x15, waiting for transfers between devices: 59.6 us -> 78.3 us  [send(): return lax.ppermute(x, AXES, [(index(*a), index(*b)) for a, b in pairs])]
  transfers between devices with their start and end apart: 15 -> 15, of which waited for: 10 -> 10; matrix products, arithmetic and copies ran while one was open for 0% -> 0% of each run, Pallas kernels for 13% -> 8%
where the time goes in v1:
time: 134 us
  waiting for transfers between devices  78.3 us (58%)
  starting transfers between devices  39.8 us (30%)
  Pallas kernels  13.3 us (10%)
    ppermute x15, waiting for transfers between devices, send(): return lax.ppermute(x, AXES, [(index(*a), index(*b)) for a, b in pairs])  78.3 us
    ppermute x15, starting transfers between devices, send(): return lax.ppermute(x, AXES, [(index(*a), index(*b)) for a, b in pairs])  39.8 us
    pallas_call x6, Pallas kernels, call(): pl.pallas_call(functools.partial(kernel, **kwargs), out_shape=out_shape,...  13.3 us
  transfers between devices with their start and end apart: 15, of which 10 were waited for; matrix products, arithmetic and copies ran while one was open for 0% of the time, Pallas kernels for 8%

profile of v1, /device:TPU:0, one launch (start us, length us, event | category | flops | bytes accessed | tf_op | source)
XLA Modules:
  0.0 133.9 jit_solution(12379056505140547905)
XLA Ops:
  0.6 1.5 %shard_map.80 = bf16[1552,512]{1,0:T(8,128)(2,1)S(1)} custom-call(s32[1]{0:T(128)} %bitcast.1.core, bf16[3072,512]{1,0:T(8,128)(2,1)} %bitcast.9, f32[2,512]{1,0:T(2,128)} %bitcast.14, f32[2,512]{1,0:T(2,128)} %bitcast.18), custom_call_target="tpu_custom_call" | custom-call | bytes 1048576 | tf_op jit(solution)/shard_map/pallas_call | solution.py:137
  2.1 0.8 collective-permute-start.6
  2.9 1.0 shard_map.77
  3.9 0.7 collective-permute-start
  4.5 1.3 collective-permute-start.1
  5.8 1.3 collective-permute-start.2
  7.1 1.3 collective-permute-start.3
  8.4 0.1 pad_add_fusion.refs_0_.place
  8.5 0.0 collective-permute-done.refs_1_
  8.5 5.5 %collective-permute-done.1.refs_2_ = bf16[144,512]{1,0:T(8,128)(2,1)} collective-permute-done((bf16[144,512]{1,0:T(8,128)(2,1)S(1)}, bf16[144,512]{1,0:T(8,128)(2,1)}, u32[]{:S(2)}, u32[]{:S(2)}) %collective-permute-start.1) | collective-permute-done | bytes 147488 | tf_op jit(solution)/shard_map/ppermute | solution.py:377
  14.0 1.4 %collective-permute-done.2.refs_3_ = bf16[144,512]{1,0:T(8,128)(2,1)} collective-permute-done((bf16[144,512]{1,0:T(8,128)(2,1)S(1)}, bf16[144,512]{1,0:T(8,128)(2,1)}, u32[]{:S(2)}, u32[]{:S(2)}) %collective-permute-start.2) | collective-permute-done | bytes 147488 | tf_op jit(solution)/shard_map/ppermute | solution.py:377
  15.4 4.7 %collective-permute-done.3.refs_4_ = bf16[144,512]{1,0:T(8,128)(2,1)} collective-permute-done((bf16[144,512]{1,0:T(8,128)(2,1)S(1)}, bf16[144,512]{1,0:T(8,128)(2,1)}, u32[]{:S(2)}, u32[]{:S(2)}) %collective-permute-start.3) | collective-permute-done | bytes 147488 | tf_op jit(solution)/shard_map/ppermute | solution.py:377
  20.1 8.6 %shard_map.78 = bf16[528,512]{1,0:T(8,128)(2,1)S(1)} custom-call(s32[3]{0:T(128)S(1)} %pad_add_fusion.refs_0_.place, bf16[144,512]{1,0:T(8,128)(2,1)S(1)} %collective-permute-done.refs_1_, bf16[144,512]{1,0:T(8,128)(2,1)} %collective-permute-done.1.refs_2_, bf16[144,512]{1,0:T(8,128)(2,1)} %collective-permute-done.2.refs_3_, ...), custom_call_target="tpu_custom_call" | custom-call | flops 2952790016 | bytes 1048576 | tf_op jit(solution)/shard_map/pallas_call | solution.py:137
  28.8 1.3 collective-permute-start.4
  30.1 12.0 %collective-permute-done.4.refs_1_ = bf16[528,512]{1,0:T(8,128)(2,1)S(1)} collective-permute-done((bf16[528,512]{1,0:T(8,128)(2,1)S(1)}, bf16[528,512]{1,0:T(8,128)(2,1)S(1)}, u32[]{:S(2)}, u32[]{:S(2)}) %collective-permute-start.4) | collective-permute-done | bytes 540704 | tf_op jit(solution)/shard_map/ppermute | solution.py:377
  42.1 0.7 shard_map.79
  42.8 0.0 collective-permute-done.6.refs_5_
  42.8 0.1 collective-permute-start.7
  42.9 0.7 collective-permute-start.5
  43.6 0.0 collective-permute-done.5.refs_1_
  43.6 2.7 %collective-permute-done.7.refs_6_ = bf16[1552,512]{1,0:T(8,128)(2,1)S(1)} collective-permute-done((bf16[1552,512]{1,0:T(8,128)(2,1)S(1)}, bf16[1552,512]{1,0:T(8,128)(2,1)S(1)}, u32[]{:S(2)}, u32[]{:S(2)}) %collective-permute-start.7) | collective-permute-done | bytes 1589280 | tf_op jit(solution)/shard_map/ppermute | solution.py:377
  46.3 0.9 shard_map.81
  47.2 29.1 %collective-permute-start.10 = (bf16[128,512]{1,0:T(8,128)(2,1)S(1)}, bf16[128,512]{1,0:T(8,128)(2,1)S(1)}, u32[]{:S(2)}, u32[]{:S(2)}) collective-permute-start(bf16[128,512]{1,0:T(8,128)(2,1)S(1)} %get-tuple-element.15), channel_id=1, source_target_pairs={{0,6},{1,7},{2,4},{3,5},{4,2},{5,3},{6,0},{7,1},{8,14},{9,15},{10,... | collective-permute-start | bytes 393224 | tf_op jit(solution)/shard_map/ppermute | solution.py:377
  76.3 0.0 collective-permute-start.8
  76.3 0.6 collective-permute-start.9
  76.9 3.7 %collective-permute-done.10.refs_3_ = bf16[128,512]{1,0:T(8,128)(2,1)S(1)} collective-permute-done((bf16[128,512]{1,0:T(8,128)(2,1)S(1)}, bf16[128,512]{1,0:T(8,128)(2,1)S(1)}, u32[]{:S(2)}, u32[]{:S(2)}) %collective-permute-start.10) | collective-permute-done | bytes 131104 | tf_op jit(solution)/shard_map/ppermute | solution.py:377
  80.6 1.5 %collective-permute-done.8.refs_1_ = bf16[128,512]{1,0:T(8,128)(2,1)S(1)} collective-permute-done((bf16[128,512]{1,0:T(8,128)(2,1)S(1)}, bf16[128,512]{1,0:T(8,128)(2,1)S(1)}, u32[]{:S(2)}, u32[]{:S(2)}) %collective-permute-start.8) | collective-permute-done | bytes 131104 | tf_op jit(solution)/shard_map/ppermute | solution.py:377
  82.2 0.7 collective-permute-done.9.refs_2_
  82.9 0.7 shard_map.82
  83.6 0.7 collective-permute-start.11
  84.3 0.7 collective-permute-start.12
  85.0 1.3 collective-permute-start.13
  86.3 0.0 collective-permute-done.11
  86.3 0.0 collective-permute-done.12
  86.3 44.7 %collective-permute-done.13 = bf16[256,512]{1,0:T(8,128)(2,1)S(1)} collective-permute-done((bf16[256,512]{1,0:T(8,128)(2,1)S(1)}, bf16[256,512]{1,0:T(8,128)(2,1)S(1)}, u32[]{:S(2)}, u32[]{:S(2)}) %collective-permute-start.13) | collective-permute-done | bytes 262176 | tf_op jit(solution)/shard_map/ppermute | solution.py:377
  131.1 0.7 fusion
  131.8 0.0 collective-permute-start.14
  131.8 1.3 %collective-permute-done.14 = bf16[128,512]{1,0:T(8,128)(2,1)S(1)} collective-permute-done((bf16[128,512]{1,0:T(8,128)(2,1)S(1)}, bf16[128,512]{1,0:T(8,128)(2,1)S(1)}, u32[]{:S(2)}, u32[]{:S(2)}) %collective-permute-start.14) | collective-permute-done | bytes 131104 | tf_op jit(solution)/shard_map/ppermute | solution.py:377
  133.1 0.7 add_multiply_fusion
  (1 shorter events, 0.0 us)
Async XLA Ops:
  2.1 40.7 %collective-permute-start.6 = (bf16[1552,512]{1,0:T(8,128)(2,1)S(1)}, bf16[1552,512]{1,0:T(8,128)(2,1)S(1)}, u32[]{:S(2)}, u32[]{:S(2)}) collective-permute-start(bf16[1552,512]{1,0:T(8,128)(2,1)S(1)} %shard_map.80), channel_id=1, source_target_pairs={{24,16},{25,17},{26,18},{27,19},{28,20},{29,21},{30,22},{31,23}} | collective-permute-start | bytes 4767752 | tf_op jit(solution)/shard_map/ppermute | solution.py:377
  3.9 4.7 %collective-permute-start = (bf16[144,512]{1,0:T(8,128)(2,1)S(1)}, bf16[144,512]{1,0:T(8,128)(2,1)S(1)}, u32[]{:S(2)}, u32[]{:S(2)}) collective-permute-start(bf16[144,512]{1,0:T(8,128)(2,1)S(1)} %shard_map.77), channel_id=1, source_target_pairs={{0,0},{1,1},{10,2},{11,3},{20,4},{21,5},{30,6},{31,7}} | collective-permute-start | bytes 442376 | tf_op jit(solution)/shard_map/ppermute | solution.py:377
  4.5 9.4 %collective-permute-start.1 = (bf16[144,512]{1,0:T(8,128)(2,1)S(1)}, bf16[144,512]{1,0:T(8,128)(2,1)}, u32[]{:S(2)}, u32[]{:S(2)}) collective-permute-start(bf16[144,512]{1,0:T(8,128)(2,1)S(1)} %shard_map.77), channel_id=1, source_target_pairs={{2,0},{3,1},{8,2},{9,3},{22,4},{23,5},{28,6},{29,7}} | collective-permute-start | bytes 442376 | tf_op jit(solution)/shard_map/ppermute | solution.py:377
  5.8 9.6 %collective-permute-start.2 = (bf16[144,512]{1,0:T(8,128)(2,1)S(1)}, bf16[144,512]{1,0:T(8,128)(2,1)}, u32[]{:S(2)}, u32[]{:S(2)}) collective-permute-start(bf16[144,512]{1,0:T(8,128)(2,1)S(1)} %shard_map.77), channel_id=1, source_target_pairs={{4,0},{5,1},{14,2},{15,3},{16,4},{17,5},{26,6},{27,7}} | collective-permute-start | bytes 442376 | tf_op jit(solution)/shard_map/ppermute | solution.py:377
  7.1 13.0 %collective-permute-start.3 = (bf16[144,512]{1,0:T(8,128)(2,1)S(1)}, bf16[144,512]{1,0:T(8,128)(2,1)}, u32[]{:S(2)}, u32[]{:S(2)}) collective-permute-start(bf16[144,512]{1,0:T(8,128)(2,1)S(1)} %shard_map.77), channel_id=1, source_target_pairs={{6,0},{7,1},{12,2},{13,3},{18,4},{19,5},{24,6},{25,7}} | collective-permute-start | bytes 442376 | tf_op jit(solution)/shard_map/ppermute | solution.py:377
  28.8 13.3 %collective-permute-start.4 = (bf16[528,512]{1,0:T(8,128)(2,1)S(1)}, bf16[528,512]{1,0:T(8,128)(2,1)S(1)}, u32[]{:S(2)}, u32[]{:S(2)}) collective-permute-start(bf16[528,512]{1,0:T(8,128)(2,1)S(1)} %shard_map.78), channel_id=1, source_target_pairs={{0,8},{1,9},{2,10},{3,11},{4,12},{5,13},{6,14},{7,15}} | collective-permute-start | bytes 1622024 | tf_op jit(solution)/shard_map/ppermute | solution.py:377
  42.8 3.5 %collective-permute-start.7 = (bf16[1552,512]{1,0:T(8,128)(2,1)S(1)}, bf16[1552,512]{1,0:T(8,128)(2,1)S(1)}, u32[]{:S(2)}, u32[]{:S(2)}) collective-permute-start(bf16[1552,512]{1,0:T(8,128)(2,1)S(1)} %collective-permute-done.6.refs_5_), channel_id=1, source_target_pairs={{0,1},{1,0},{2,3},{3,2},{4,5},{5,4},{6,7},{7,6},{8,9},{9,8},{10,11... | collective-permute-start | bytes 4767752 | tf_op jit(solution)/shard_map/ppermute | solution.py:377
  42.9 0.7 collective-permute-start.5
  47.2 33.5 %collective-permute-start.10 = (bf16[128,512]{1,0:T(8,128)(2,1)S(1)}, bf16[128,512]{1,0:T(8,128)(2,1)S(1)}, u32[]{:S(2)}, u32[]{:S(2)}) collective-permute-start(bf16[128,512]{1,0:T(8,128)(2,1)S(1)} %get-tuple-element.15), channel_id=1, source_target_pairs={{0,6},{1,7},{2,4},{3,5},{4,2},{5,3},{6,0},{7,1},{8,14},{9,15},{10,... | collective-permute-start | bytes 393224 | tf_op jit(solution)/shard_map/ppermute | solution.py:377
  76.3 5.9 %collective-permute-start.8 = (bf16[128,512]{1,0:T(8,128)(2,1)S(1)}, bf16[128,512]{1,0:T(8,128)(2,1)S(1)}, u32[]{:S(2)}, u32[]{:S(2)}) collective-permute-start(bf16[128,512]{1,0:T(8,128)(2,1)S(1)} %get-tuple-element.13), channel_id=1, source_target_pairs={{0,2},{1,3},{2,0},{3,1},{4,6},{5,7},{6,4},{7,5},{8,10},{9,11},{10,... | collective-permute-start | bytes 393224 | tf_op jit(solution)/shard_map/ppermute | solution.py:377
  76.3 6.6 %collective-permute-start.9 = (bf16[128,512]{1,0:T(8,128)(2,1)S(1)}, bf16[128,512]{1,0:T(8,128)(2,1)S(1)}, u32[]{:S(2)}, u32[]{:S(2)}) collective-permute-start(bf16[128,512]{1,0:T(8,128)(2,1)S(1)} %get-tuple-element.14), channel_id=1, source_target_pairs={{0,4},{1,5},{2,6},{3,7},{4,0},{5,1},{6,2},{7,3},{8,12},{9,13},{10,... | collective-permute-start | bytes 393224 | tf_op jit(solution)/shard_map/ppermute | solution.py:377
  83.6 2.7 %collective-permute-start.11 = (bf16[256,512]{1,0:T(8,128)(2,1)S(1)}, bf16[256,512]{1,0:T(8,128)(2,1)S(1)}, u32[]{:S(2)}, u32[]{:S(2)}) collective-permute-start(bf16[256,512]{1,0:T(8,128)(2,1)S(1)} %get-tuple-element.16), channel_id=1, source_target_pairs={{16,24},{17,25},{18,26},{19,27},{20,28},{21,29},{22,30},{23,31}} | collective-permute-start | bytes 786440 | tf_op jit(solution)/shard_map/ppermute | solution.py:377
  84.3 2.0 %collective-permute-start.12 = (bf16[256,512]{1,0:T(8,128)(2,1)S(1)}, bf16[256,512]{1,0:T(8,128)(2,1)S(1)}, u32[]{:S(2)}, u32[]{:S(2)}) collective-permute-start(bf16[256,512]{1,0:T(8,128)(2,1)S(1)} %get-tuple-element.17), channel_id=1, source_target_pairs={{16,8},{17,9},{18,10},{19,11},{20,12},{21,13},{22,14},{23,15}} | collective-permute-start | bytes 786440 | tf_op jit(solution)/shard_map/ppermute | solution.py:377
  85.0 46.0 %collective-permute-start.13 = (bf16[256,512]{1,0:T(8,128)(2,1)S(1)}, bf16[256,512]{1,0:T(8,128)(2,1)S(1)}, u32[]{:S(2)}, u32[]{:S(2)}) collective-permute-start(bf16[256,512]{1,0:T(8,128)(2,1)S(1)} %get-tuple-element.18), channel_id=1, source_target_pairs={{16,0},{17,1},{18,2},{19,3},{20,4},{21,5},{22,6},{23,7}} | collective-permute-start | bytes 786440 | tf_op jit(solution)/shard_map/ppermute | solution.py:377
  131.8 1.3 %collective-permute-start.14 = (bf16[128,512]{1,0:T(8,128)(2,1)S(1)}, bf16[128,512]{1,0:T(8,128)(2,1)S(1)}, u32[]{:S(2)}, u32[]{:S(2)}) collective-permute-start(bf16[128,512]{1,0:T(8,128)(2,1)S(1)} %get-tuple-element.20), channel_id=1, source_target_pairs={{0,1},{1,0},{2,3},{3,2},{4,5},{5,4},{6,7},{7,6},{8,9},{9,8},{10,11... | collective-permute-start | bytes 393224 | tf_op jit(solution)/shard_map/ppermute | solution.py:377

commit v2 on v1

--- a/solution.py
+++ b/solution.py
@@ -203,28 +203,19 @@
     if given:
         parts, refs = refs[:2], refs[2:]
     outs, refs = (refs[:4], refs[4:]) if split else (refs[:1], refs[1:])
-    loaded, own_terms, riders, senders, hidden, words, table, sems = refs[:8]
+    loaded, riders, senders, hidden, words, table, sems = refs[:7]
     width = senders.shape[2]
     nodes = 4 * BLK
     d, e = place[0], place[1]
     part = MATS * width // 4
     half = 2 * part
-    plans = [
-        [
-            pltpu.make_async_copy(biases, own_terms.at[pl.ds(0, 2), :], sems.at[14]),
-            pltpu.make_async_copy(gains, own_terms.at[pl.ds(2, 2), :], sems.at[15]),
-        ]
-        + [
-            pltpu.make_async_copy(mats.at[pl.ds(i * width, width), :], loaded.at[0, pl.ds(i * width, width), :], sems.at[i])
-            for i in range(MATS)
-        ]
-    ]
+    plans = [[]]
     if given:
         plans.append(
             [
                 pltpu.make_async_copy(
                     x.at[pl.ds(0, half), :],
-                    loaded.at[1, pl.ds(pl.multiple_of(row * half, BLK), half), :],
+                    loaded.at[pl.ds(pl.multiple_of(row * half, BLK), half), :],
                     sems.at[6 + i],
                 )
                 for i, (x, row) in enumerate(zip(parts, (e, 1 - e)))
@@ -236,12 +227,12 @@
             copy.start()
 
     if fresh:
-        copies = [pltpu.make_async_copy(x, refs[8].at[r], sems.at[10 + r]) for r, x in enumerate(inputs)]
+        copies = [pltpu.make_async_copy(x, refs[7].at[r], sems.at[10 + r]) for r, x in enumerate(inputs)]
         for copy in copies:
             copy.start()
         for copy in copies:
             copy.wait()
-        inputs = [refs[8].at[r] for r in range(4)]
+        inputs = [refs[7].at[r] for r in range(4)]
         state = jnp.concatenate([x[0:BLK] for x in inputs], axis=0)
         rows = []
         for r in range(4):
@@ -259,22 +250,17 @@
     for at, copies in enumerate(plans):
         last_layer = at == len(plans) - 1
         if at == 0:
-            copies[0].wait()
-            copies[1].wait()
-            terms = own_terms[...]
-            matrix_copies = copies[2:]
+            terms = jnp.concatenate([biases[...], gains[...]], axis=0)
+            source = mats
         else:
             for copy in copies:
                 copy.wait()
             values = riders[...].astype(F32)
             terms = values[0:4] + values[4:8] + values[8:12]
-            matrix_copies = None
+            source = loaded
 
         def mat(i):
-            if matrix_copies and matrix_copies[i] is not None:
-                matrix_copies[i].wait()
-                matrix_copies[i] = None
-            return loaded[at, i * width : (i + 1) * width, :]
+            return source[i * width : (i + 1) * width, :]
 
         sent = dot(state, mat(0)).astype(BF16).astype(F32)
         for b in range(4):
@@ -310,9 +296,9 @@
 
 def run_layers(place, where, inputs, slots, own, given=None, split=False):
     width = inputs[0].shape[1]
-    smem, vmem, hbm = pltpu.SMEM, pltpu.VMEM, pltpu.HBM
+    smem, vmem = pltpu.SMEM, pltpu.VMEM
     fresh = len(inputs) == 4
-    args, spaces = [place] + inputs + list(own), [smem] + [pl.ANY if fresh else vmem] * len(inputs) + [hbm] * 3
+    args, spaces = [place] + inputs + list(own), [smem] + [pl.ANY if fresh else vmem] * len(inputs) + [vmem] * 3
     if given:
         args, spaces = args + list(given), spaces + [pl.ANY] * 2
     layers = 1 if given is None else 2
@@ -324,8 +310,7 @@
         args,
         spaces,
         scratch=[
-            pltpu.VMEM((layers, MATS * width, width), BF16),
-            pltpu.VMEM((4, width), F32),
+            pltpu.VMEM((MATS * width if given else 16, width), BF16),
             pltpu.VMEM((RIDERS, width), BF16),
             pltpu.VMEM((4, 2 * BLK + 8, width), F32),
             pltpu.VMEM((4, slots * BLK, width), BF16),

time: 134 us -> 130 us (0.970)
  waiting for transfers between devices: 78.3 us -> 74.7 us
    ppermute x15, waiting for transfers between devices: 78.3 us -> 74.7 us  [send(): return lax.ppermute(x, AXES, [(index(*a), index(*b)) for a, b in pairs])]
  transfers between devices with their start and end apart: 15 -> 15, of which waited for: 10 -> 10; matrix products, arithmetic and copies ran while one was open for 0% -> 0% of each run, Pallas kernels for 8% -> 7%
where the time goes in v2:
time: 130 us
  waiting for transfers between devices  74.7 us (57%)
  starting transfers between devices  40.1 us (31%)
  Pallas kernels  13 us (10%)
    ppermute x15, waiting for transfers between devices, send(): return lax.ppermute(x, AXES, [(index(*a), index(*b)) for a, b in pairs])  74.7 us
    ppermute x15, starting transfers between devices, send(): return lax.ppermute(x, AXES, [(index(*a), index(*b)) for a, b in pairs])  40.1 us
    pallas_call x6, Pallas kernels, call(): pl.pallas_call(functools.partial(kernel, **kwargs), out_shape=out_shape,...  13 us
  transfers between devices with their start and end apart: 15, of which 10 were waited for; matrix products, arithmetic and copies ran while one was open for 0% of the time, Pallas kernels for 7%

profile of v2, /device:TPU:0, one launch (start us, length us, event | category | flops | bytes accessed | tf_op | source)
XLA Modules:
  0.0 130.2 jit_solution(172838360243708373)
XLA Ops:
  0.6 0.0 copy-start
  0.6 0.0 copy-start.1
  0.7 0.0 copy-start.2
  0.7 2.8 %shard_map.80 = bf16[1552,512]{1,0:T(8,128)(2,1)} custom-call(s32[1]{0:T(128)} %bitcast.1.core, bf16[3072,512]{1,0:T(8,128)(2,1)} %bitcast.9, f32[2,512]{1,0:T(2,128)} %bitcast.13, f32[2,512]{1,0:T(2,128)} %bitcast.17), custom_call_target="tpu_custom_call" | custom-call | bytes 1048576 | tf_op jit(solution)/shard_map/pallas_call | solution.py:137
  3.5 1.8 %collective-permute-start.6 = (bf16[1552,512]{1,0:T(8,128)(2,1)}, bf16[1552,512]{1,0:T(8,128)(2,1)}, u32[]{:S(2)}, u32[]{:S(2)}) collective-permute-start(bf16[1552,512]{1,0:T(8,128)(2,1)} %shard_map.80), channel_id=1, source_target_pairs={{24,16},{25,17},{26,18},{27,19},{28,20},{29,21},{30,22},{31,23}} | collective-permute-start | bytes 4767752 | tf_op jit(solution)/shard_map/ppermute | solution.py:362
  5.3 1.0 shard_map.77
  6.2 0.7 collective-permute-start
  6.9 1.3 collective-permute-start.1
  8.2 1.3 collective-permute-start.2
  9.5 1.3 collective-permute-start.3
  10.8 0.1 pad_add_fusion.refs_0_.place
  10.9 0.0 collective-permute-done.refs_1_
  10.9 5.5 %collective-permute-done.1.refs_2_ = bf16[144,512]{1,0:T(8,128)(2,1)} collective-permute-done((bf16[144,512]{1,0:T(8,128)(2,1)S(1)}, bf16[144,512]{1,0:T(8,128)(2,1)}, u32[]{:S(2)}, u32[]{:S(2)}) %collective-permute-start.1) | collective-permute-done | bytes 147488 | tf_op jit(solution)/shard_map/ppermute | solution.py:362
  16.4 1.4 %collective-permute-done.2.refs_3_ = bf16[144,512]{1,0:T(8,128)(2,1)} collective-permute-done((bf16[144,512]{1,0:T(8,128)(2,1)S(1)}, bf16[144,512]{1,0:T(8,128)(2,1)}, u32[]{:S(2)}, u32[]{:S(2)}) %collective-permute-start.2) | collective-permute-done | bytes 147488 | tf_op jit(solution)/shard_map/ppermute | solution.py:362
  17.8 4.7 %collective-permute-done.3.refs_4_ = bf16[144,512]{1,0:T(8,128)(2,1)} collective-permute-done((bf16[144,512]{1,0:T(8,128)(2,1)S(1)}, bf16[144,512]{1,0:T(8,128)(2,1)}, u32[]{:S(2)}, u32[]{:S(2)}) %collective-permute-start.3) | collective-permute-done | bytes 147488 | tf_op jit(solution)/shard_map/ppermute | solution.py:362
  22.5 0.0 copy-done
  22.5 0.0 copy-done.1
  22.5 0.0 copy-done.2
  22.5 7.0 %shard_map.78 = bf16[528,512]{1,0:T(8,128)(2,1)S(1)} custom-call(s32[3]{0:T(128)S(1)} %pad_add_fusion.refs_0_.place, bf16[144,512]{1,0:T(8,128)(2,1)S(1)} %collective-permute-done.refs_1_, bf16[144,512]{1,0:T(8,128)(2,1)} %collective-permute-done.1.refs_2_, bf16[144,512]{1,0:T(8,128)(2,1)} %collective-permute-done.2.refs_3_, ...), custom_call_target="tpu_custom_call" | custom-call | flops 2952790016 | bytes 1048576 | tf_op jit(solution)/shard_map/pallas_call | solution.py:137
  29.6 1.3 %collective-permute-start.4 = (bf16[528,512]{1,0:T(8,128)(2,1)S(1)}, bf16[528,512]{1,0:T(8,128)(2,1)S(1)}, u32[]{:S(2)}, u32[]{:S(2)}) collective-permute-start(bf16[528,512]{1,0:T(8,128)(2,1)S(1)} %shard_map.78), channel_id=1, source_target_pairs={{0,8},{1,9},{2,10},{3,11},{4,12},{5,13},{6,14},{7,15}} | collective-permute-start | bytes 1622024 | tf_op jit(solution)/shard_map/ppermute | solution.py:362
  30.9 12.0 %collective-permute-done.4.refs_1_ = bf16[528,512]{1,0:T(8,128)(2,1)S(1)} collective-permute-done((bf16[528,512]{1,0:T(8,128)(2,1)S(1)}, bf16[528,512]{1,0:T(8,128)(2,1)S(1)}, u32[]{:S(2)}, u32[]{:S(2)}) %collective-permute-start.4) | collective-permute-done | bytes 540704 | tf_op jit(solution)/shard_map/ppermute | solution.py:362
  42.9 0.7 shard_map.79
  43.6 0.0 collective-permute-done.6.refs_5_
  43.6 0.1 collective-permute-start.7
  43.6 0.7 collective-permute-start.5
  44.3 0.0 collective-permute-done.5.refs_1_
  44.4 2.9 %collective-permute-done.7.refs_6_ = bf16[1552,512]{1,0:T(8,128)(2,1)S(1)} collective-permute-done((bf16[1552,512]{1,0:T(8,128)(2,1)}, bf16[1552,512]{1,0:T(8,128)(2,1)S(1)}, u32[]{:S(2)}, u32[]{:S(2)}) %collective-permute-start.7) | collective-permute-done | bytes 1589280 | tf_op jit(solution)/shard_map/ppermute | solution.py:362
  47.3 0.9 shard_map.81
  48.2 28.3 %collective-permute-start.10 = (bf16[128,512]{1,0:T(8,128)(2,1)S(1)}, bf16[128,512]{1,0:T(8,128)(2,1)S(1)}, u32[]{:S(2)}, u32[]{:S(2)}) collective-permute-start(bf16[128,512]{1,0:T(8,128)(2,1)S(1)} %get-tuple-element.15), channel_id=1, source_target_pairs={{0,6},{1,7},{2,4},{3,5},{4,2},{5,3},{6,0},{7,1},{8,14},{9,15},{10,... | collective-permute-start | bytes 393224 | tf_op jit(solution)/shard_map/ppermute | solution.py:362
  76.5 0.0 collective-permute-start.8
  76.5 0.6 collective-permute-start.9
  77.1 3.7 %collective-permute-done.10.refs_3_ = bf16[128,512]{1,0:T(8,128)(2,1)S(1)} collective-permute-done((bf16[128,512]{1,0:T(8,128)(2,1)S(1)}, bf16[128,512]{1,0:T(8,128)(2,1)S(1)}, u32[]{:S(2)}, u32[]{:S(2)}) %collective-permute-start.10) | collective-permute-done | bytes 131104 | tf_op jit(solution)/shard_map/ppermute | solution.py:362
  80.8 1.5 %collective-permute-done.8.refs_1_ = bf16[128,512]{1,0:T(8,128)(2,1)S(1)} collective-permute-done((bf16[128,512]{1,0:T(8,128)(2,1)S(1)}, bf16[128,512]{1,0:T(8,128)(2,1)S(1)}, u32[]{:S(2)}, u32[]{:S(2)}) %collective-permute-start.8) | collective-permute-done | bytes 131104 | tf_op jit(solution)/shard_map/ppermute | solution.py:362
  82.4 0.7 collective-permute-done.9.refs_2_
  83.1 0.7 shard_map.82
  83.8 0.7 collective-permute-start.11
  84.5 0.7 collective-permute-start.12
  85.2 1.3 collective-permute-start.13
  86.5 0.0 collective-permute-done.11
  86.5 0.0 collective-permute-done.12
  86.5 40.8 %collective-permute-done.13 = bf16[256,512]{1,0:T(8,128)(2,1)S(1)} collective-permute-done((bf16[256,512]{1,0:T(8,128)(2,1)S(1)}, bf16[256,512]{1,0:T(8,128)(2,1)S(1)}, u32[]{:S(2)}, u32[]{:S(2)}) %collective-permute-start.13) | collective-permute-done | bytes 262176 | tf_op jit(solution)/shard_map/ppermute | solution.py:362
  127.4 0.7 fusion
  128.1 0.0 collective-permute-start.14
  128.1 1.3 %collective-permute-done.14 = bf16[128,512]{1,0:T(8,128)(2,1)S(1)} collective-permute-done((bf16[128,512]{1,0:T(8,128)(2,1)S(1)}, bf16[128,512]{1,0:T(8,128)(2,1)S(1)}, u32[]{:S(2)}, u32[]{:S(2)}) %collective-permute-start.14) | collective-permute-done | bytes 131104 | tf_op jit(solution)/shard_map/ppermute | solution.py:362
  129.4 0.7 add_multiply_fusion
  (1 shorter events, 0.0 us)
Async XLA Ops:
  0.6 21.9 %copy-start = (bf16[1,6,512,512]{3,2,1,0:T(8,128)(2,1)S(1)}, bf16[1,6,512,512]{3,2,1,0:T(8,128)(2,1)}, u32[]{:S(2)}) copy-start(bf16[1,6,512,512]{3,2,1,0:T(8,128)(2,1)} %param.7) | copy-start | bytes 9437188
  0.6 21.9 %copy-start.1 = (f32[1,2,512]{2,1,0:T(2,128)S(1)}, f32[1,2,512]{2,1,0:T(2,128)}, u32[]{:S(2)}) copy-start(f32[1,2,512]{2,1,0:T(2,128)} %param.8) | copy-start | bytes 12292
  0.7 21.9 %copy-start.2 = (f32[1,2,512]{2,1,0:T(2,128)S(1)}, f32[1,2,512]{2,1,0:T(2,128)}, u32[]{:S(2)}) copy-start(f32[1,2,512]{2,1,0:T(2,128)} %param.9) | copy-start | bytes 12292
  3.5 40.1 %collective-permute-start.6 = (bf16[1552,512]{1,0:T(8,128)(2,1)}, bf16[1552,512]{1,0:T(8,128)(2,1)}, u32[]{:S(2)}, u32[]{:S(2)}) collective-permute-start(bf16[1552,512]{1,0:T(8,128)(2,1)} %shard_map.80), channel_id=1, source_target_pairs={{24,16},{25,17},{26,18},{27,19},{28,20},{29,21},{30,22},{31,23}} | collective-permute-start | bytes 4767752 | tf_op jit(solution)/shard_map/ppermute | solution.py:362
  6.2 4.7 %collective-permute-start = (bf16[144,512]{1,0:T(8,128)(2,1)S(1)}, bf16[144,512]{1,0:T(8,128)(2,1)S(1)}, u32[]{:S(2)}, u32[]{:S(2)}) collective-permute-start(bf16[144,512]{1,0:T(8,128)(2,1)S(1)} %shard_map.77), channel_id=1, source_target_pairs={{0,0},{1,1},{10,2},{11,3},{20,4},{21,5},{30,6},{31,7}} | collective-permute-start | bytes 442376 | tf_op jit(solution)/shard_map/ppermute | solution.py:362
  6.9 9.4 %collective-permute-start.1 = (bf16[144,512]{1,0:T(8,128)(2,1)S(1)}, bf16[144,512]{1,0:T(8,128)(2,1)}, u32[]{:S(2)}, u32[]{:S(2)}) collective-permute-start(bf16[144,512]{1,0:T(8,128)(2,1)S(1)} %shard_map.77), channel_id=1, source_target_pairs={{2,0},{3,1},{8,2},{9,3},{22,4},{23,5},{28,6},{29,7}} | collective-permute-start | bytes 442376 | tf_op jit(solution)/shard_map/ppermute | solution.py:362
  8.2 9.6 %collective-permute-start.2 = (bf16[144,512]{1,0:T(8,128)(2,1)S(1)}, bf16[144,512]{1,0:T(8,128)(2,1)}, u32[]{:S(2)}, u32[]{:S(2)}) collective-permute-start(bf16[144,512]{1,0:T(8,128)(2,1)S(1)} %shard_map.77), channel_id=1, source_target_pairs={{4,0},{5,1},{14,2},{15,3},{16,4},{17,5},{26,6},{27,7}} | collective-permute-start | bytes 442376 | tf_op jit(solution)/shard_map/ppermute | solution.py:362
  9.5 13.0 %collective-permute-start.3 = (bf16[144,512]{1,0:T(8,128)(2,1)S(1)}, bf16[144,512]{1,0:T(8,128)(2,1)}, u32[]{:S(2)}, u32[]{:S(2)}) collective-permute-start(bf16[144,512]{1,0:T(8,128)(2,1)S(1)} %shard_map.77), channel_id=1, source_target_pairs={{6,0},{7,1},{12,2},{13,3},{18,4},{19,5},{24,6},{25,7}} | collective-permute-start | bytes 442376 | tf_op jit(solution)/shard_map/ppermute | solution.py:362
  29.6 13.3 %collective-permute-start.4 = (bf16[528,512]{1,0:T(8,128)(2,1)S(1)}, bf16[528,512]{1,0:T(8,128)(2,1)S(1)}, u32[]{:S(2)}, u32[]{:S(2)}) collective-permute-start(bf16[528,512]{1,0:T(8,128)(2,1)S(1)} %shard_map.78), channel_id=1, source_target_pairs={{0,8},{1,9},{2,10},{3,11},{4,12},{5,13},{6,14},{7,15}} | collective-permute-start | bytes 1622024 | tf_op jit(solution)/shard_map/ppermute | solution.py:362
  43.6 3.7 %collective-permute-start.7 = (bf16[1552,512]{1,0:T(8,128)(2,1)}, bf16[1552,512]{1,0:T(8,128)(2,1)S(1)}, u32[]{:S(2)}, u32[]{:S(2)}) collective-permute-start(bf16[1552,512]{1,0:T(8,128)(2,1)} %collective-permute-done.6.refs_5_), channel_id=1, source_target_pairs={{0,1},{1,0},{2,3},{3,2},{4,5},{5,4},{6,7},{7,6},{8,9},{9,8},{10,11... | collective-permute-start | bytes 4767752 | tf_op jit(solution)/shard_map/ppermute | solution.py:362
  43.6 0.7 collective-permute-start.5
  48.2 32.7 %collective-permute-start.10 = (bf16[128,512]{1,0:T(8,128)(2,1)S(1)}, bf16[128,512]{1,0:T(8,128)(2,1)S(1)}, u32[]{:S(2)}, u32[]{:S(2)}) collective-permute-start(bf16[128,512]{1,0:T(8,128)(2,1)S(1)} %get-tuple-element.15), channel_id=1, source_target_pairs={{0,6},{1,7},{2,4},{3,5},{4,2},{5,3},{6,0},{7,1},{8,14},{9,15},{10,... | collective-permute-start | bytes 393224 | tf_op jit(solution)/shard_map/ppermute | solution.py:362
  76.5 5.9 %collective-permute-start.8 = (bf16[128,512]{1,0:T(8,128)(2,1)S(1)}, bf16[128,512]{1,0:T(8,128)(2,1)S(1)}, u32[]{:S(2)}, u32[]{:S(2)}) collective-permute-start(bf16[128,512]{1,0:T(8,128)(2,1)S(1)} %get-tuple-element.13), channel_id=1, source_target_pairs={{0,2},{1,3},{2,0},{3,1},{4,6},{5,7},{6,4},{7,5},{8,10},{9,11},{10,... | collective-permute-start | bytes 393224 | tf_op jit(solution)/shard_map/ppermute | solution.py:362
  76.5 6.6 %collective-permute-start.9 = (bf16[128,512]{1,0:T(8,128)(2,1)S(1)}, bf16[128,512]{1,0:T(8,128)(2,1)S(1)}, u32[]{:S(2)}, u32[]{:S(2)}) collective-permute-start(bf16[128,512]{1,0:T(8,128)(2,1)S(1)} %get-tuple-element.14), channel_id=1, source_target_pairs={{0,4},{1,5},{2,6},{3,7},{4,0},{5,1},{6,2},{7,3},{8,12},{9,13},{10,... | collective-permute-start | bytes 393224 | tf_op jit(solution)/shard_map/ppermute | solution.py:362
  83.8 2.7 %collective-permute-start.11 = (bf16[256,512]{1,0:T(8,128)(2,1)S(1)}, bf16[256,512]{1,0:T(8,128)(2,1)S(1)}, u32[]{:S(2)}, u32[]{:S(2)}) collective-permute-start(bf16[256,512]{1,0:T(8,128)(2,1)S(1)} %get-tuple-element.16), channel_id=1, source_target_pairs={{16,24},{17,25},{18,26},{19,27},{20,28},{21,29},{22,30},{23,31}} | collective-permute-start | bytes 786440 | tf_op jit(solution)/shard_map/ppermute | solution.py:362
  84.5 2.0 %collective-permute-start.12 = (bf16[256,512]{1,0:T(8,128)(2,1)S(1)}, bf16[256,512]{1,0:T(8,128)(2,1)S(1)}, u32[]{:S(2)}, u32[]{:S(2)}) collective-permute-start(bf16[256,512]{1,0:T(8,128)(2,1)S(1)} %get-tuple-element.17), channel_id=1, source_target_pairs={{16,8},{17,9},{18,10},{19,11},{20,12},{21,13},{22,14},{23,15}} | collective-permute-start | bytes 786440 | tf_op jit(solution)/shard_map/ppermute | solution.py:362
  85.2 42.2 %collective-permute-start.13 = (bf16[256,512]{1,0:T(8,128)(2,1)S(1)}, bf16[256,512]{1,0:T(8,128)(2,1)S(1)}, u32[]{:S(2)}, u32[]{:S(2)}) collective-permute-start(bf16[256,512]{1,0:T(8,128)(2,1)S(1)} %get-tuple-element.18), channel_id=1, source_target_pairs={{16,0},{17,1},{18,2},{19,3},{20,4},{21,5},{22,6},{23,7}} | collective-permute-start | bytes 786440 | tf_op jit(solution)/shard_map/ppermute | solution.py:362
  128.1 1.3 %collective-permute-start.14 = (bf16[128,512]{1,0:T(8,128)(2,1)S(1)}, bf16[128,512]{1,0:T(8,128)(2,1)S(1)}, u32[]{:S(2)}, u32[]{:S(2)}) collective-permute-start(bf16[128,512]{1,0:T(8,128)(2,1)S(1)} %get-tuple-element.20), channel_id=1, source_target_pairs={{0,1},{1,0},{2,3},{3,2},{4,5},{5,4},{6,7},{7,6},{8,9},{9,8},{10,11... | collective-permute-start | bytes 393224 | tf_op jit(solution)/shard_map/ppermute | solution.py:362
